TPU v7x, 32 devices: a whole 2x2x4 slice. The times are simulated.
32 devices in a mesh: blk: 8 (over z, y), beam: 4 (over x, core).
Axes of the slice: x: 2, y: 2, z: 4, core: 2. Of those that a mesh axis runs over, the one named last changes fastest.
Arguments:
- signal: float32 [524288], P(('blk', 'beam')), may hold values from -6 to 6
- weight: float32 [524288], P(('blk', 'beam')), may hold values from 0.25 to 1
- cycle: int32 [524288], P(('blk', 'beam')), may hold values from 0 to 1
- phi: int32 [524288], P(('blk', 'beam')), may hold values from 0 to 2047
- psi: int32 [524288], P(('blk', 'beam')), may hold values from 0 to 31
- owner: int32 [4096, 1], P(('blk', 'beam')), may hold values from 0 to 7; in each aligned block of 128 rows (0 to 127, 128 to 255, ...) at most 40 rows name the same one
- wigner: bfloat16 [1024, 32, 16, 1152], P('blk', 'beam'), may hold values from -0.375 to 0.375
Outputs:
- alm: float32 [1024, 2, 1152], P(('blk', 'beam'))
Inputs may be any that keep to these rules, and one draw needn't show every extreme that they name: `owner`: among the 128 blocks of one device no cycle group is named by more than 40 blocks, and in some device's blocks one group is named by exactly 40.
All inputs are finite; a program needn't handle non-finite values.
Results may differ from a plain program's by a relative error of at most 0.02.
Values may be sent and summed in bfloat16 or wider, within the bound.
No kernel may reach another device: no remote copies, remote signals or barrier semaphores. Data moves between devices by JAX's collectives and lax.ppermute only.
A program may use at most 128 MiB of HBM per device.

v0:
```python
import math
import jax
import jax.numpy as jnp
from jax import lax
from jax.sharding import PartitionSpec as P

BLOCK_ROWS = 128
CYCLE_DEV = 2
NPSI = 32
NPHI = 2048


def psi_rows(psi_index, length):
    component = jnp.arange(length, dtype=jnp.int32)[:, None]
    middle = length // 2
    frequency = jnp.where(component <= middle, component, component - middle)
    residue = (frequency * psi_index[None, :] % length).astype(jnp.float32)
    angles = residue * jnp.float32(2.0 * math.pi / length)
    return jnp.where(component <= middle, jnp.cos(angles), jnp.sin(angles)) * jnp.float32(
        1.0 / math.sqrt(length)
    )


def phi_table(length):
    cell_index = jnp.arange(length, dtype=jnp.int32)[:, None]
    column = jnp.arange(length, dtype=jnp.int32)[None, :]
    residue = (column // 2 * cell_index % length).astype(jnp.float32)
    angles = residue * jnp.float32(2.0 * math.pi / length)
    values = jnp.where(column % 2 == 0, jnp.cos(angles), jnp.sin(angles)) * jnp.float32(
        1.0 / math.sqrt(length)
    )
    return values.astype(jnp.bfloat16)


def block_turns(total):
    turns = max(1, total // 2048)
    while total % turns != 0:
        turns = turns - 1
    return turns


def shards(signal, weight, cycle, phi, psi, owner, wigner):
    groups = lax.axis_size("blk")
    beams = lax.axis_size("beam")
    blocks = owner.shape[0]
    capacity = max(2, 5 * blocks // (2 * groups))
    slots = capacity * BLOCK_ROWS
    target_group = owner[:, 0]
    hits = (target_group[:, None] == jnp.arange(groups, dtype=jnp.int32)[None, :]).astype(jnp.int32)
    earlier = jnp.cumsum(hits, axis=0) - hits
    within = jnp.sum(earlier * hits, axis=1)
    position = target_group * capacity + within
    source = (
        jnp.zeros((groups * capacity,), jnp.int32)
        .at[position]
        .set(jnp.arange(blocks, dtype=jnp.int32))
    )
    filled = jnp.zeros((groups * capacity,), jnp.int32).at[position].set(1)

    def arrange(data):
        leading = data.shape[0]
        shaped = data.reshape(leading, blocks, BLOCK_ROWS)
        taken = jnp.take(shaped, source, axis=1)
        taken = jnp.where(filled[None, :, None] > 0, taken, jnp.zeros_like(taken))
        return taken.reshape(leading, groups, slots)

    sample_value = signal * weight
    packed = (cycle * NPSI + psi) * NPHI + phi
    total = groups * slots
    got_value, got_code = (
        lax.all_to_all(
            arrange(sample_value[None, :]).astype(jnp.bfloat16),
            "blk",
            split_axis=1,
            concat_axis=1,
            tiled=True,
        ).astype(jnp.float32),
        lax.all_to_all(arrange(packed[None, :]), "blk", split_axis=1, concat_axis=1, tiled=True),
    )
    codes = got_code.reshape(total)
    arrived = got_value.reshape(total)
    received = (psi_rows(codes // NPHI % NPSI, NPSI) * arrived[None, :]).astype(jnp.bfloat16)
    cycle_of = codes // (NPSI * NPHI)
    phi_of = codes % NPHI
    spread = jnp.concatenate(
        [
            jnp.where(cycle_of[None, :] == level, received, jnp.zeros_like(received))
            for level in range(CYCLE_DEV)
        ],
        axis=0,
    )
    turns = block_turns(total)
    width = total // turns
    columns = jnp.arange(NPHI, dtype=jnp.int32)

    def bin_block(number, carry):
        start = number * width
        part = lax.dynamic_slice_in_dim(spread, start, width, 1)
        place = lax.dynamic_slice_in_dim(phi_of, start, width, 0)
        onehot = (place[:, None] == columns[None, :]).astype(jnp.bfloat16)
        return carry + jnp.dot(part, onehot, preferred_element_type=jnp.float32)

    cube = lax.fori_loop(0, turns, bin_block, jnp.zeros((CYCLE_DEV * NPSI, NPHI), jnp.float32))
    cube = cube.reshape(CYCLE_DEV, NPSI, NPHI)
    share = NPSI // beams
    summed = lax.psum(cube.astype(jnp.bfloat16), "beam").astype(jnp.float32)
    mine = lax.dynamic_slice_in_dim(summed, lax.axis_index("beam") * share, share, 1)
    spectra = jnp.dot(
        mine.astype(jnp.bfloat16).reshape(CYCLE_DEV * share, NPHI),
        phi_table(NPHI),
        preferred_element_type=jnp.float32,
    )
    spectra = spectra.astype(jnp.bfloat16).reshape(CYCLE_DEV, share, NPHI)
    regrouped = lax.all_to_all(spectra, "blk", split_axis=2, concat_axis=0, tiled=True)
    orders = regrouped.shape[2] // 2
    coeffs = regrouped.reshape(regrouped.shape[0], share, orders, 2).transpose(2, 1, 0, 3)
    partial_sum = jnp.einsum("mqtl,mqtp->mpl", wigner, coeffs, preferred_element_type=jnp.float32)
    totals = lax.psum(partial_sum.astype(jnp.bfloat16), "beam").astype(jnp.float32)
    return lax.dynamic_slice_in_dim(
        totals, lax.axis_index("beam") * (orders // beams), orders // beams, 0
    )


def solution(mesh):
    return jax.shard_map(
        shards,
        mesh=mesh,
        in_specs=(
            P(("blk", "beam")),
            P(("blk", "beam")),
            P(("blk", "beam")),
            P(("blk", "beam")),
            P(("blk", "beam")),
            P(("blk", "beam"), None),
            P("blk", "beam", None, None),
        ),
        out_specs=P(("blk", "beam"), None, None),
        check_vma=False,
    )
```

profile of v0, /device:TPU:0, one launch (start us, length us, event | category | flops | bytes accessed | tf_op | source)
XLA Modules:
  0.0 333.1 jit_solution(5072294114963490575)
XLA Ops:
  6.5 0.7 fusion.35
  7.4 0.8 select_reduce_fusion
  8.3 0.7 fusion.46
  9.0 1.0 scatter_custom_fusion.1
  10.2 1.0 scatter_custom_fusion
  11.3 0.9 multiply_bitcast_fusion
  12.2 1.4 gather_fusion.1
  14.4 1.1 reduce
  16.1 7.3 %all-to-all-start.1 = ((bf16[8,2,2560]{2,1,0:T(2,128)(2,1)}), bf16[8,2,2560]{2,1,0:T(2,128)(2,1)S(1)}, u32[]{:S(2)}, u32[]{:S(2)}) async-start(bf16[8,2,2560]{2,1,0:T(2,128)(2,1)} %reshape.312), calls=%async_computation.1 | async-start | bytes 163840 | tf_op jit(solution)/shard_map/all_to_all | solution.py:71
  23.5 0.9 add_bitcast_fusion
  24.4 1.1 gather_fusion
  25.6 0.8 copy.17
  26.4 4.1 %all-to-all-done.1 = bf16[8,2,2560]{2,1,0:T(2,128)(2,1)S(1)} async-done(((bf16[8,2,2560]{2,1,0:T(2,128)(2,1)}), bf16[8,2,2560]{2,1,0:T(2,128)(2,1)S(1)}, u32[]{:S(2)}, u32[]{:S(2)}) %all-to-all-start.1) | async-done | bytes 81952 | tf_op jit(solution)/shard_map/all_to_all | solution.py:71
  30.5 3.4 %all-to-all-start = ((s32[1,8,5120]{2,0,1:T(1,128)}), s32[1,8,5120]{2,0,1:T(1,128)S(1)}, u32[]{:S(2)}, u32[]{:S(2)}) async-start(s32[1,8,5120]{2,0,1:T(1,128)} %copy.17), calls=%async_computation | async-start | bytes 327680 | tf_op jit(solution)/shard_map/all_to_all | solution.py:78
  34.4 7.0 %all-to-all-done = s32[1,8,5120]{2,0,1:T(1,128)S(1)} async-done(((s32[1,8,5120]{2,0,1:T(1,128)}), s32[1,8,5120]{2,0,1:T(1,128)S(1)}, u32[]{:S(2)}, u32[]{:S(2)}) %all-to-all-start) | async-done | bytes 163872 | tf_op jit(solution)/shard_map/all_to_all | solution.py:78
  41.7 21.8 %broadcast_select_fusion.1 = (bf16[32,40960]{1,0:T(8,128)(2,1)S(1)}, bf16[32,40960]{1,0:T(8,128)(2,1)S(1)}) fusion(pred[40960]{0:T(1024)(128)(4,1)S(1)} %get-tuple-element.129, f32[40960]{0:T(1024)S(1)} %bitcast.53, s32[40960]{0:T(1024)S(1)} %get-tuple-element.128, s32[32]{0:T(128)S(1)} %add_select_fusion.8, pred[32]{0:T(512)(128)(4,1)S(1)} %iota_compare_fusion.5, ...), kind=kLoop, calls=%fused_computation.37 | loop fusion | flops 24903680 | bytes 5652640 | tf_op jit(solution)/shard_map/jit(_where)/select_n | solution.py:87
  63.6 2.7 pad_maximum_fusion
  66.2 90.4 %while.14 = (s32[]{:T(128)}, f32[64,2048]{1,0:T(8,128)S(1)}, bf16[64,40960]{1,0:T(8,128)(2,1)}, s32[40960]{0:T(1024)S(1)}, s32[]{:T(128)}, /*index=5*/s32[]{:T(128)}, s32[]{:T(128)}, s32[]{:T(128)}) while((s32[]{:T(128)}, f32[64,2048]{1,0:T(8,128)S(1)}, bf16[64,40960]{1,0:T(8,128)(2,1)}, s32[40960]{0:T(1024)S(1)}, s32[]{:T(128)}, ...), condition=%wide.region_5.6_spmd.clone, body=%wide.region_4.5_spmd.clone.sunk | while | flops 541327360 | bytes 1335445 | solution.py:103
  66.2 4.5 %fusion.59 = f32[64,2048]{1,0:T(8,128)S(1)} fusion(s32[2048]{0:T(1024)S(1)} %dynamic_slice.39, f32[64,2048]{1,0:T(8,128)S(1)} %get-tuple-element.165, bf16[64,40960]{1,0:T(8,128)(2,1)} %get-tuple-element.174, s32[]{:T(128)S(6)} %select_n.263, pred[]{:T(512)S(6)} %compare.34), kind=kOutput, calls=%fused_computation.8.clone.1 | convolution fusion | flops 541327360 | bytes 1318917 | tf_op jit(solution)/shard_map/while/body/eval_jaxpr/dot_general | solution.py:101
  70.7 4.5 %fusion.59 = f32[64,2048]{1,0:T(8,128)S(1)} fusion(s32[2048]{0:T(1024)S(1)} %dynamic_slice.39, f32[64,2048]{1,0:T(8,128)S(1)} %get-tuple-element.165, bf16[64,40960]{1,0:T(8,128)(2,1)} %get-tuple-element.174, s32[]{:T(128)S(6)} %select_n.263, pred[]{:T(512)S(6)} %compare.34), kind=kOutput, calls=%fused_computation.8.clone.1 | convolution fusion | flops 541327360 | bytes 1318917 | tf_op jit(solution)/shard_map/while/body/eval_jaxpr/dot_general | solution.py:101
  75.3 4.5 %fusion.59 = f32[64,2048]{1,0:T(8,128)S(1)} fusion(s32[2048]{0:T(1024)S(1)} %dynamic_slice.39, f32[64,2048]{1,0:T(8,128)S(1)} %get-tuple-element.165, bf16[64,40960]{1,0:T(8,128)(2,1)} %get-tuple-element.174, s32[]{:T(128)S(6)} %select_n.263, pred[]{:T(512)S(6)} %compare.34), kind=kOutput, calls=%fused_computation.8.clone.1 | convolution fusion | flops 541327360 | bytes 1318917 | tf_op jit(solution)/shard_map/while/body/eval_jaxpr/dot_general | solution.py:101
  79.8 4.5 %fusion.59 = f32[64,2048]{1,0:T(8,128)S(1)} fusion(s32[2048]{0:T(1024)S(1)} %dynamic_slice.39, f32[64,2048]{1,0:T(8,128)S(1)} %get-tuple-element.165, bf16[64,40960]{1,0:T(8,128)(2,1)} %get-tuple-element.174, s32[]{:T(128)S(6)} %select_n.263, pred[]{:T(512)S(6)} %compare.34), kind=kOutput, calls=%fused_computation.8.clone.1 | convolution fusion | flops 541327360 | bytes 1318917 | tf_op jit(solution)/shard_map/while/body/eval_jaxpr/dot_general | solution.py:101
  84.3 4.5 %fusion.59 = f32[64,2048]{1,0:T(8,128)S(1)} fusion(s32[2048]{0:T(1024)S(1)} %dynamic_slice.39, f32[64,2048]{1,0:T(8,128)S(1)} %get-tuple-element.165, bf16[64,40960]{1,0:T(8,128)(2,1)} %get-tuple-element.174, s32[]{:T(128)S(6)} %select_n.263, pred[]{:T(512)S(6)} %compare.34), kind=kOutput, calls=%fused_computation.8.clone.1 | convolution fusion | flops 541327360 | bytes 1318917 | tf_op jit(solution)/shard_map/while/body/eval_jaxpr/dot_general | solution.py:101
  88.8 4.5 %fusion.59 = f32[64,2048]{1,0:T(8,128)S(1)} fusion(s32[2048]{0:T(1024)S(1)} %dynamic_slice.39, f32[64,2048]{1,0:T(8,128)S(1)} %get-tuple-element.165, bf16[64,40960]{1,0:T(8,128)(2,1)} %get-tuple-element.174, s32[]{:T(128)S(6)} %select_n.263, pred[]{:T(512)S(6)} %compare.34), kind=kOutput, calls=%fused_computation.8.clone.1 | convolution fusion | flops 541327360 | bytes 1318917 | tf_op jit(solution)/shard_map/while/body/eval_jaxpr/dot_general | solution.py:101
  93.3 4.5 %fusion.59 = f32[64,2048]{1,0:T(8,128)S(1)} fusion(s32[2048]{0:T(1024)S(1)} %dynamic_slice.39, f32[64,2048]{1,0:T(8,128)S(1)} %get-tuple-element.165, bf16[64,40960]{1,0:T(8,128)(2,1)} %get-tuple-element.174, s32[]{:T(128)S(6)} %select_n.263, pred[]{:T(512)S(6)} %compare.34), kind=kOutput, calls=%fused_computation.8.clone.1 | convolution fusion | flops 541327360 | bytes 1318917 | tf_op jit(solution)/shard_map/while/body/eval_jaxpr/dot_general | solution.py:101
  97.9 4.5 %fusion.59 = f32[64,2048]{1,0:T(8,128)S(1)} fusion(s32[2048]{0:T(1024)S(1)} %dynamic_slice.39, f32[64,2048]{1,0:T(8,128)S(1)} %get-tuple-element.165, bf16[64,40960]{1,0:T(8,128)(2,1)} %get-tuple-element.174, s32[]{:T(128)S(6)} %select_n.263, pred[]{:T(512)S(6)} %compare.34), kind=kOutput, calls=%fused_computation.8.clone.1 | convolution fusion | flops 541327360 | bytes 1318917 | tf_op jit(solution)/shard_map/while/body/eval_jaxpr/dot_general | solution.py:101
  102.4 4.5 %fusion.59 = f32[64,2048]{1,0:T(8,128)S(1)} fusion(s32[2048]{0:T(1024)S(1)} %dynamic_slice.39, f32[64,2048]{1,0:T(8,128)S(1)} %get-tuple-element.165, bf16[64,40960]{1,0:T(8,128)(2,1)} %get-tuple-element.174, s32[]{:T(128)S(6)} %select_n.263, pred[]{:T(512)S(6)} %compare.34), kind=kOutput, calls=%fused_computation.8.clone.1 | convolution fusion | flops 541327360 | bytes 1318917 | tf_op jit(solution)/shard_map/while/body/eval_jaxpr/dot_general | solution.py:101
  106.9 4.5 %fusion.59 = f32[64,2048]{1,0:T(8,128)S(1)} fusion(s32[2048]{0:T(1024)S(1)} %dynamic_slice.39, f32[64,2048]{1,0:T(8,128)S(1)} %get-tuple-element.165, bf16[64,40960]{1,0:T(8,128)(2,1)} %get-tuple-element.174, s32[]{:T(128)S(6)} %select_n.263, pred[]{:T(512)S(6)} %compare.34), kind=kOutput, calls=%fused_computation.8.clone.1 | convolution fusion | flops 541327360 | bytes 1318917 | tf_op jit(solution)/shard_map/while/body/eval_jaxpr/dot_general | solution.py:101
  111.4 4.5 %fusion.59 = f32[64,2048]{1,0:T(8,128)S(1)} fusion(s32[2048]{0:T(1024)S(1)} %dynamic_slice.39, f32[64,2048]{1,0:T(8,128)S(1)} %get-tuple-element.165, bf16[64,40960]{1,0:T(8,128)(2,1)} %get-tuple-element.174, s32[]{:T(128)S(6)} %select_n.263, pred[]{:T(512)S(6)} %compare.34), kind=kOutput, calls=%fused_computation.8.clone.1 | convolution fusion | flops 541327360 | bytes 1318917 | tf_op jit(solution)/shard_map/while/body/eval_jaxpr/dot_general | solution.py:101
  116.0 4.5 %fusion.59 = f32[64,2048]{1,0:T(8,128)S(1)} fusion(s32[2048]{0:T(1024)S(1)} %dynamic_slice.39, f32[64,2048]{1,0:T(8,128)S(1)} %get-tuple-element.165, bf16[64,40960]{1,0:T(8,128)(2,1)} %get-tuple-element.174, s32[]{:T(128)S(6)} %select_n.263, pred[]{:T(512)S(6)} %compare.34), kind=kOutput, calls=%fused_computation.8.clone.1 | convolution fusion | flops 541327360 | bytes 1318917 | tf_op jit(solution)/shard_map/while/body/eval_jaxpr/dot_general | solution.py:101
  120.5 4.5 %fusion.59 = f32[64,2048]{1,0:T(8,128)S(1)} fusion(s32[2048]{0:T(1024)S(1)} %dynamic_slice.39, f32[64,2048]{1,0:T(8,128)S(1)} %get-tuple-element.165, bf16[64,40960]{1,0:T(8,128)(2,1)} %get-tuple-element.174, s32[]{:T(128)S(6)} %select_n.263, pred[]{:T(512)S(6)} %compare.34), kind=kOutput, calls=%fused_computation.8.clone.1 | convolution fusion | flops 541327360 | bytes 1318917 | tf_op jit(solution)/shard_map/while/body/eval_jaxpr/dot_general | solution.py:101
  125.0 4.5 %fusion.59 = f32[64,2048]{1,0:T(8,128)S(1)} fusion(s32[2048]{0:T(1024)S(1)} %dynamic_slice.39, f32[64,2048]{1,0:T(8,128)S(1)} %get-tuple-element.165, bf16[64,40960]{1,0:T(8,128)(2,1)} %get-tuple-element.174, s32[]{:T(128)S(6)} %select_n.263, pred[]{:T(512)S(6)} %compare.34), kind=kOutput, calls=%fused_computation.8.clone.1 | convolution fusion | flops 541327360 | bytes 1318917 | tf_op jit(solution)/shard_map/while/body/eval_jaxpr/dot_general | solution.py:101
  129.5 4.5 %fusion.59 = f32[64,2048]{1,0:T(8,128)S(1)} fusion(s32[2048]{0:T(1024)S(1)} %dynamic_slice.39, f32[64,2048]{1,0:T(8,128)S(1)} %get-tuple-element.165, bf16[64,40960]{1,0:T(8,128)(2,1)} %get-tuple-element.174, s32[]{:T(128)S(6)} %select_n.263, pred[]{:T(512)S(6)} %compare.34), kind=kOutput, calls=%fused_computation.8.clone.1 | convolution fusion | flops 541327360 | bytes 1318917 | tf_op jit(solution)/shard_map/while/body/eval_jaxpr/dot_general | solution.py:101
  134.0 4.5 %fusion.59 = f32[64,2048]{1,0:T(8,128)S(1)} fusion(s32[2048]{0:T(1024)S(1)} %dynamic_slice.39, f32[64,2048]{1,0:T(8,128)S(1)} %get-tuple-element.165, bf16[64,40960]{1,0:T(8,128)(2,1)} %get-tuple-element.174, s32[]{:T(128)S(6)} %select_n.263, pred[]{:T(512)S(6)} %compare.34), kind=kOutput, calls=%fused_computation.8.clone.1 | convolution fusion | flops 541327360 | bytes 1318917 | tf_op jit(solution)/shard_map/while/body/eval_jaxpr/dot_general | solution.py:101
  138.6 4.5 %fusion.59 = f32[64,2048]{1,0:T(8,128)S(1)} fusion(s32[2048]{0:T(1024)S(1)} %dynamic_slice.39, f32[64,2048]{1,0:T(8,128)S(1)} %get-tuple-element.165, bf16[64,40960]{1,0:T(8,128)(2,1)} %get-tuple-element.174, s32[]{:T(128)S(6)} %select_n.263, pred[]{:T(512)S(6)} %compare.34), kind=kOutput, calls=%fused_computation.8.clone.1 | convolution fusion | flops 541327360 | bytes 1318917 | tf_op jit(solution)/shard_map/while/body/eval_jaxpr/dot_general | solution.py:101
  143.1 4.5 %fusion.59 = f32[64,2048]{1,0:T(8,128)S(1)} fusion(s32[2048]{0:T(1024)S(1)} %dynamic_slice.39, f32[64,2048]{1,0:T(8,128)S(1)} %get-tuple-element.165, bf16[64,40960]{1,0:T(8,128)(2,1)} %get-tuple-element.174, s32[]{:T(128)S(6)} %select_n.263, pred[]{:T(512)S(6)} %compare.34), kind=kOutput, calls=%fused_computation.8.clone.1 | convolution fusion | flops 541327360 | bytes 1318917 | tf_op jit(solution)/shard_map/while/body/eval_jaxpr/dot_general | solution.py:101
  147.6 4.5 %fusion.59 = f32[64,2048]{1,0:T(8,128)S(1)} fusion(s32[2048]{0:T(1024)S(1)} %dynamic_slice.39, f32[64,2048]{1,0:T(8,128)S(1)} %get-tuple-element.165, bf16[64,40960]{1,0:T(8,128)(2,1)} %get-tuple-element.174, s32[]{:T(128)S(6)} %select_n.263, pred[]{:T(512)S(6)} %compare.34), kind=kOutput, calls=%fused_computation.8.clone.1 | convolution fusion | flops 541327360 | bytes 1318917 | tf_op jit(solution)/shard_map/while/body/eval_jaxpr/dot_general | solution.py:101
  152.1 4.5 %fusion.59 = f32[64,2048]{1,0:T(8,128)S(1)} fusion(s32[2048]{0:T(1024)S(1)} %dynamic_slice.39, f32[64,2048]{1,0:T(8,128)S(1)} %get-tuple-element.165, bf16[64,40960]{1,0:T(8,128)(2,1)} %get-tuple-element.174, s32[]{:T(128)S(6)} %select_n.263, pred[]{:T(512)S(6)} %compare.34), kind=kOutput, calls=%fused_computation.8.clone.1 | convolution fusion | flops 541327360 | bytes 1318917 | tf_op jit(solution)/shard_map/while/body/eval_jaxpr/dot_general | solution.py:101
  156.6 0.7 convert_element_type.58
  157.7 30.0 %all-reduce.3.cloned.1.call-done = bf16[2,32,2048]{2,1,0:T(8,128)(2,1)} async-done(((bf16[2,32,2048]{2,1,0:T(8,128)(2,1)}), bf16[2,32,2048]{2,1,0:T(8,128)(2,1)}) %all-reduce.3.cloned.1.call-update) | async-done | bytes 262160 | tf_op jit(solution)/shard_map/psum | solution.py:106
  187.7 68.3 %fusion.27 = bf16[2,8,2048]{2,1,0:T(8,128)(2,1)S(1)} fusion(s32[2048]{0:T(1024)S(1)} %add_select_fusion.6, pred[2048]{0:T(1024)(128)(4,1)S(1)} %fusion.36, bf16[2,32,2048]{2,1,0:T(8,128)(2,1)} %all-reduce.3.cloned.1.call-done, s32[]{:T(128)S(6)} %select_n.186), kind=kOutput, calls=%fused_computation.40 | convolution fusion | flops 205619200 | bytes 141316 | tf_op jit(solution)/shard_map/dot_general | solution.py:108
  256.0 0.8 copy.19
  256.8 1.1 reshape.314
  257.8 12.2 %all_to_all.25 = bf16[8,2,2048]{2,1,0:T(2,128)(2,1)S(1)} all-to-all(bf16[8,2,2048]{2,1,0:T(2,128)(2,1)S(1)} %reshape.314), channel_id=1, replica_groups=mesh['blk'=8,'beam'=4] {'blk'}, dimensions={0} | all-to-all | bytes 131072 | tf_op jit(solution)/shard_map/all_to_all | solution.py:114
  270.0 1.2 reshape.315
  271.5 22.5 %fusion.23 = bf16[128,2,1152]{2,1,0:T(2,128)(2,1)} fusion(bf16[128,8,16,2]{1,3,0,2:T(2,128)(2,1)S(1)} %bitcast.52, bf16[128,8,16,1152]{3,2,1,0:T(8,128)(2,1)} %param.15), kind=kOutput, calls=%fused_computation.38 | convolution fusion | flops 75792384 | bytes 38404096 | tf_op jit(solution)/shard_map/mqtl,mqtp->mpl/dot_general | solution.py:117
  294.0 30.5 %all-reduce.5.cloned.1.call-done = bf16[128,2,1152]{2,1,0:T(2,128)(2,1)} async-done(((bf16[128,2,1152]{2,1,0:T(2,128)(2,1)}), bf16[128,2,1152]{2,1,0:T(2,128)(2,1)}) %all-reduce.5.cloned.1.call-update) | async-done | bytes 589840 | tf_op jit(solution)/shard_map/psum | solution.py:118
  324.5 1.7 dynamic-slice_convert_fusion
  (52 shorter events, 3.5 us)
Async XLA Ops:
  16.1 14.3 %all-to-all-start.1 = ((bf16[8,2,2560]{2,1,0:T(2,128)(2,1)}), bf16[8,2,2560]{2,1,0:T(2,128)(2,1)S(1)}, u32[]{:S(2)}, u32[]{:S(2)}) async-start(bf16[8,2,2560]{2,1,0:T(2,128)(2,1)} %reshape.312), calls=%async_computation.1 | async-start | bytes 163840 | tf_op jit(solution)/shard_map/all_to_all | solution.py:71
  30.5 10.9 %all-to-all-start = ((s32[1,8,5120]{2,0,1:T(1,128)}), s32[1,8,5120]{2,0,1:T(1,128)S(1)}, u32[]{:S(2)}, u32[]{:S(2)}) async-start(s32[1,8,5120]{2,0,1:T(1,128)} %copy.17), calls=%async_computation | async-start | bytes 327680 | tf_op jit(solution)/shard_map/all_to_all | solution.py:78
  33.9 153.8 %all-reduce.3.cloned.1.call-start = ((), (), s32[]{:S(2)}) async-start(), calls=%async_computation.3 | async-start | bytes 524288 | tf_op jit(solution)/shard_map/psum | solution.py:106
  157.4 167.1 %all-reduce.5.cloned.1.call-start = ((), (), s32[]{:S(2)}) async-start(), calls=%async_computation.4 | async-start | bytes 1179648 | tf_op jit(solution)/shard_map/psum | solution.py:118
Sparse Core Ops, SparseCore 0:
  157.5 30.1 all-reduce.2
  294.1 30.3 all-reduce.4
where the time goes:
time: 334 us; the launch traced here: 333 us
  matrix products  180 us (54%)
  waiting for transfers between devices  71.6 us (21%)
  other arithmetic  33 us (10%)
  between operations  13.7 us (4%)
  blocking collectives  12.2 us (4%)
  starting transfers between devices  11.2 us (3%)
  local copies, waits for them, and re-layouts  10.4 us (3%)
    dot_general x20, matrix products, bin_block(): return carry + jnp.dot(part, onehot, preferred_element_type=jnp.float32)  89.4 us
    dot_general x1, matrix products, shards(): jnp.dot(mine.astype(jnp.bfloat16).reshape(CYCLE_DEV * share, NPHI), phi_t...  68.3 us
    psum x1, waiting for transfers between devices, shards(): lax.psum(partial_sum.astype(jnp.bfloat16), 'beam').astype(jnp.float32)  30.5 us
    psum x1, waiting for transfers between devices, shards(): summed = lax.psum(cube.astype(jnp.bfloat16), 'beam').astype(jnp.float32)  30 us
    dot_general x1, matrix products, shards(): jnp.einsum('mqtl,mqtp->mpl', wigner, coeffs, preferred_element_type=jnp.f...  22.5 us
    select_n x1, other arithmetic, shards(): jnp.where(cycle_of[None, :] == level, received, jnp.zeros_like(received))  21.8 us
    all_to_all x1, blocking collectives, shards(): lax.all_to_all(spectra, 'blk', split_axis=2, concat_axis=0, tiled=True)  12.2 us
    all_to_all x1, starting transfers between devices, shards(): lax.all_to_all(arrange(sample_value[None, :]).astype(jnp.bfloat16), 'blk'...  7.31 us
  transfers between devices with their start and end apart: 4, of which 4 were waited for; matrix products, arithmetic and copies ran while one was open for 1% of the time, Pallas kernels for 0%

commit v1 on v0

--- a/solution.py
+++ b/solution.py
@@ -103,7 +103,7 @@
     cube = lax.fori_loop(0, turns, bin_block, jnp.zeros((CYCLE_DEV * NPSI, NPHI), jnp.float32))
     cube = cube.reshape(CYCLE_DEV, NPSI, NPHI)
     share = NPSI // beams
-    summed = lax.psum(cube.astype(jnp.bfloat16), "beam").astype(jnp.float32)
+    summed = jnp.sum(lax.all_gather(cube.astype(jnp.bfloat16), "beam"), axis=0).astype(jnp.float32)
     mine = lax.dynamic_slice_in_dim(summed, lax.axis_index("beam") * share, share, 1)
     spectra = jnp.dot(
         mine.astype(jnp.bfloat16).reshape(CYCLE_DEV * share, NPHI),

time: 334 us -> 319 us (0.955)
  waiting for transfers between devices: 71.6 us -> 56 us
    psum x1 -> x0, waiting for transfers between devices: 30 us -> none  [shards(): summed = lax.psum(cube.astype(jnp.bfloat16), 'beam').astype(jnp.float32)]
    all_gather x0 -> x1, waiting for transfers between devices: none -> 14.4 us  [shards(): lax.all_gather(cube.astype(jnp.bfloat16), 'beam')]
where the time goes in v1:
time: 319 us; the launch traced here: 318 us
  matrix products  179 us (56%)
  waiting for transfers between devices  56 us (18%)
  other arithmetic  34.4 us (11%)
  between operations  13.7 us (4%)
  blocking collectives  12.2 us (4%)
  starting transfers between devices  11.2 us (4%)
  local copies, waits for them, and re-layouts  10.4 us (3%)
    dot_general x20, matrix products, bin_block(): return carry + jnp.dot(part, onehot, preferred_element_type=jnp.float32)  89.5 us
    dot_general x1, matrix products, shards(): jnp.dot(mine.astype(jnp.bfloat16).reshape(CYCLE_DEV * share, NPHI), phi_t...  67.5 us
    psum x1, waiting for transfers between devices, shards(): lax.psum(partial_sum.astype(jnp.bfloat16), 'beam').astype(jnp.float32)  30.6 us
    dot_general x1, matrix products, shards(): jnp.einsum('mqtl,mqtp->mpl', wigner, coeffs, preferred_element_type=jnp.f...  22.5 us
    select_n x1, other arithmetic, shards(): jnp.where(cycle_of[None, :] == level, received, jnp.zeros_like(received))  21.8 us
    all_gather x1, waiting for transfers between devices, shards(): lax.all_gather(cube.astype(jnp.bfloat16), 'beam')  14.4 us
    all_to_all x1, blocking collectives, shards(): lax.all_to_all(spectra, 'blk', split_axis=2, concat_axis=0, tiled=True)  12.2 us
    all_to_all x1, starting transfers between devices, shards(): lax.all_to_all(arrange(sample_value[None, :]).astype(jnp.bfloat16), 'blk'...  7.31 us
  transfers between devices with their start and end apart: 4, of which 4 were waited for; matrix products, arithmetic and copies ran while one was open for 1% of the time, Pallas kernels for 0%

profile of v1, /device:TPU:0, one launch (start us, length us, event | category | flops | bytes accessed | tf_op | source)
XLA Modules:
  0.0 318.1 jit_solution(14300442300268046084)
XLA Ops:
  6.5 0.7 fusion.35
  7.4 0.8 select_reduce_fusion
  9.0 1.0 scatter_custom_fusion.1
  10.2 1.0 scatter_custom_fusion
  11.3 0.9 multiply_bitcast_fusion
  12.2 1.4 gather_fusion.1
  14.4 1.1 reduce.1
  16.1 7.3 %all-to-all-start.1 = ((bf16[8,2,2560]{2,1,0:T(2,128)(2,1)}), bf16[8,2,2560]{2,1,0:T(2,128)(2,1)S(1)}, u32[]{:S(2)}, u32[]{:S(2)}) async-start(bf16[8,2,2560]{2,1,0:T(2,128)(2,1)} %reshape.322), calls=%async_computation.1 | async-start | bytes 163840 | tf_op jit(solution)/shard_map/all_to_all | solution.py:71
  23.5 0.9 add_bitcast_fusion
  24.4 1.1 gather_fusion
  25.6 0.8 copy.17
  26.4 4.1 %all-to-all-done.1 = bf16[8,2,2560]{2,1,0:T(2,128)(2,1)S(1)} async-done(((bf16[8,2,2560]{2,1,0:T(2,128)(2,1)}), bf16[8,2,2560]{2,1,0:T(2,128)(2,1)S(1)}, u32[]{:S(2)}, u32[]{:S(2)}) %all-to-all-start.1) | async-done | bytes 81952 | tf_op jit(solution)/shard_map/all_to_all | solution.py:71
  30.5 3.4 %all-to-all-start = ((s32[1,8,5120]{2,0,1:T(1,128)}), s32[1,8,5120]{2,0,1:T(1,128)S(1)}, u32[]{:S(2)}, u32[]{:S(2)}) async-start(s32[1,8,5120]{2,0,1:T(1,128)} %copy.17), calls=%async_computation | async-start | bytes 327680 | tf_op jit(solution)/shard_map/all_to_all | solution.py:78
  34.4 7.0 %all-to-all-done = s32[1,8,5120]{2,0,1:T(1,128)S(1)} async-done(((s32[1,8,5120]{2,0,1:T(1,128)}), s32[1,8,5120]{2,0,1:T(1,128)S(1)}, u32[]{:S(2)}, u32[]{:S(2)}) %all-to-all-start) | async-done | bytes 163872 | tf_op jit(solution)/shard_map/all_to_all | solution.py:78
  41.7 21.8 %broadcast_select_fusion.1 = (bf16[32,40960]{1,0:T(8,128)(2,1)S(1)}, bf16[32,40960]{1,0:T(8,128)(2,1)S(1)}) fusion(pred[40960]{0:T(1024)(128)(4,1)S(1)} %get-tuple-element.129, f32[40960]{0:T(1024)S(1)} %bitcast.53, s32[40960]{0:T(1024)S(1)} %get-tuple-element.128, s32[32]{0:T(128)S(1)} %add_select_fusion.8, pred[32]{0:T(512)(128)(4,1)S(1)} %iota_compare_fusion.5, ...), kind=kLoop, calls=%fused_computation.37 | loop fusion | flops 24903680 | bytes 5652640 | tf_op jit(solution)/shard_map/jit(_where)/select_n | solution.py:87
  63.6 2.7 pad_maximum_fusion
  66.2 90.4 %while.14 = (s32[]{:T(128)}, f32[64,2048]{1,0:T(8,128)S(1)}, bf16[64,40960]{1,0:T(8,128)(2,1)}, s32[40960]{0:T(1024)S(1)}, s32[]{:T(128)}, /*index=5*/s32[]{:T(128)}, s32[]{:T(128)}, s32[]{:T(128)}) while((s32[]{:T(128)}, f32[64,2048]{1,0:T(8,128)S(1)}, bf16[64,40960]{1,0:T(8,128)(2,1)}, s32[40960]{0:T(1024)S(1)}, s32[]{:T(128)}, ...), condition=%wide.region_5.6_spmd.clone, body=%wide.region_4.5_spmd.clone.sunk | while | flops 541327360 | bytes 1335445 | solution.py:103
  66.2 4.5 %fusion.59 = f32[64,2048]{1,0:T(8,128)S(1)} fusion(s32[2048]{0:T(1024)S(1)} %dynamic_slice.39, f32[64,2048]{1,0:T(8,128)S(1)} %get-tuple-element.165, bf16[64,40960]{1,0:T(8,128)(2,1)} %get-tuple-element.174, s32[]{:T(128)S(6)} %select_n.263, pred[]{:T(512)S(6)} %compare.34), kind=kOutput, calls=%fused_computation.8.clone.1 | convolution fusion | flops 541327360 | bytes 1318917 | tf_op jit(solution)/shard_map/while/body/eval_jaxpr/dot_general | solution.py:101
  70.7 4.5 %fusion.59 = f32[64,2048]{1,0:T(8,128)S(1)} fusion(s32[2048]{0:T(1024)S(1)} %dynamic_slice.39, f32[64,2048]{1,0:T(8,128)S(1)} %get-tuple-element.165, bf16[64,40960]{1,0:T(8,128)(2,1)} %get-tuple-element.174, s32[]{:T(128)S(6)} %select_n.263, pred[]{:T(512)S(6)} %compare.34), kind=kOutput, calls=%fused_computation.8.clone.1 | convolution fusion | flops 541327360 | bytes 1318917 | tf_op jit(solution)/shard_map/while/body/eval_jaxpr/dot_general | solution.py:101
  75.3 4.5 %fusion.59 = f32[64,2048]{1,0:T(8,128)S(1)} fusion(s32[2048]{0:T(1024)S(1)} %dynamic_slice.39, f32[64,2048]{1,0:T(8,128)S(1)} %get-tuple-element.165, bf16[64,40960]{1,0:T(8,128)(2,1)} %get-tuple-element.174, s32[]{:T(128)S(6)} %select_n.263, pred[]{:T(512)S(6)} %compare.34), kind=kOutput, calls=%fused_computation.8.clone.1 | convolution fusion | flops 541327360 | bytes 1318917 | tf_op jit(solution)/shard_map/while/body/eval_jaxpr/dot_general | solution.py:101
  79.8 4.5 %fusion.59 = f32[64,2048]{1,0:T(8,128)S(1)} fusion(s32[2048]{0:T(1024)S(1)} %dynamic_slice.39, f32[64,2048]{1,0:T(8,128)S(1)} %get-tuple-element.165, bf16[64,40960]{1,0:T(8,128)(2,1)} %get-tuple-element.174, s32[]{:T(128)S(6)} %select_n.263, pred[]{:T(512)S(6)} %compare.34), kind=kOutput, calls=%fused_computation.8.clone.1 | convolution fusion | flops 541327360 | bytes 1318917 | tf_op jit(solution)/shard_map/while/body/eval_jaxpr/dot_general | solution.py:101
  84.3 4.5 %fusion.59 = f32[64,2048]{1,0:T(8,128)S(1)} fusion(s32[2048]{0:T(1024)S(1)} %dynamic_slice.39, f32[64,2048]{1,0:T(8,128)S(1)} %get-tuple-element.165, bf16[64,40960]{1,0:T(8,128)(2,1)} %get-tuple-element.174, s32[]{:T(128)S(6)} %select_n.263, pred[]{:T(512)S(6)} %compare.34), kind=kOutput, calls=%fused_computation.8.clone.1 | convolution fusion | flops 541327360 | bytes 1318917 | tf_op jit(solution)/shard_map/while/body/eval_jaxpr/dot_general | solution.py:101
  88.8 4.5 %fusion.59 = f32[64,2048]{1,0:T(8,128)S(1)} fusion(s32[2048]{0:T(1024)S(1)} %dynamic_slice.39, f32[64,2048]{1,0:T(8,128)S(1)} %get-tuple-element.165, bf16[64,40960]{1,0:T(8,128)(2,1)} %get-tuple-element.174, s32[]{:T(128)S(6)} %select_n.263, pred[]{:T(512)S(6)} %compare.34), kind=kOutput, calls=%fused_computation.8.clone.1 | convolution fusion | flops 541327360 | bytes 1318917 | tf_op jit(solution)/shard_map/while/body/eval_jaxpr/dot_general | solution.py:101
  93.3 4.5 %fusion.59 = f32[64,2048]{1,0:T(8,128)S(1)} fusion(s32[2048]{0:T(1024)S(1)} %dynamic_slice.39, f32[64,2048]{1,0:T(8,128)S(1)} %get-tuple-element.165, bf16[64,40960]{1,0:T(8,128)(2,1)} %get-tuple-element.174, s32[]{:T(128)S(6)} %select_n.263, pred[]{:T(512)S(6)} %compare.34), kind=kOutput, calls=%fused_computation.8.clone.1 | convolution fusion | flops 541327360 | bytes 1318917 | tf_op jit(solution)/shard_map/while/body/eval_jaxpr/dot_general | solution.py:101
  97.9 4.5 %fusion.59 = f32[64,2048]{1,0:T(8,128)S(1)} fusion(s32[2048]{0:T(1024)S(1)} %dynamic_slice.39, f32[64,2048]{1,0:T(8,128)S(1)} %get-tuple-element.165, bf16[64,40960]{1,0:T(8,128)(2,1)} %get-tuple-element.174, s32[]{:T(128)S(6)} %select_n.263, pred[]{:T(512)S(6)} %compare.34), kind=kOutput, calls=%fused_computation.8.clone.1 | convolution fusion | flops 541327360 | bytes 1318917 | tf_op jit(solution)/shard_map/while/body/eval_jaxpr/dot_general | solution.py:101
  102.4 4.5 %fusion.59 = f32[64,2048]{1,0:T(8,128)S(1)} fusion(s32[2048]{0:T(1024)S(1)} %dynamic_slice.39, f32[64,2048]{1,0:T(8,128)S(1)} %get-tuple-element.165, bf16[64,40960]{1,0:T(8,128)(2,1)} %get-tuple-element.174, s32[]{:T(128)S(6)} %select_n.263, pred[]{:T(512)S(6)} %compare.34), kind=kOutput, calls=%fused_computation.8.clone.1 | convolution fusion | flops 541327360 | bytes 1318917 | tf_op jit(solution)/shard_map/while/body/eval_jaxpr/dot_general | solution.py:101
  106.9 4.5 %fusion.59 = f32[64,2048]{1,0:T(8,128)S(1)} fusion(s32[2048]{0:T(1024)S(1)} %dynamic_slice.39, f32[64,2048]{1,0:T(8,128)S(1)} %get-tuple-element.165, bf16[64,40960]{1,0:T(8,128)(2,1)} %get-tuple-element.174, s32[]{:T(128)S(6)} %select_n.263, pred[]{:T(512)S(6)} %compare.34), kind=kOutput, calls=%fused_computation.8.clone.1 | convolution fusion | flops 541327360 | bytes 1318917 | tf_op jit(solution)/shard_map/while/body/eval_jaxpr/dot_general | solution.py:101
  111.4 4.5 %fusion.59 = f32[64,2048]{1,0:T(8,128)S(1)} fusion(s32[2048]{0:T(1024)S(1)} %dynamic_slice.39, f32[64,2048]{1,0:T(8,128)S(1)} %get-tuple-element.165, bf16[64,40960]{1,0:T(8,128)(2,1)} %get-tuple-element.174, s32[]{:T(128)S(6)} %select_n.263, pred[]{:T(512)S(6)} %compare.34), kind=kOutput, calls=%fused_computation.8.clone.1 | convolution fusion | flops 541327360 | bytes 1318917 | tf_op jit(solution)/shard_map/while/body/eval_jaxpr/dot_general | solution.py:101
  116.0 4.5 %fusion.59 = f32[64,2048]{1,0:T(8,128)S(1)} fusion(s32[2048]{0:T(1024)S(1)} %dynamic_slice.39, f32[64,2048]{1,0:T(8,128)S(1)} %get-tuple-element.165, bf16[64,40960]{1,0:T(8,128)(2,1)} %get-tuple-element.174, s32[]{:T(128)S(6)} %select_n.263, pred[]{:T(512)S(6)} %compare.34), kind=kOutput, calls=%fused_computation.8.clone.1 | convolution fusion | flops 541327360 | bytes 1318917 | tf_op jit(solution)/shard_map/while/body/eval_jaxpr/dot_general | solution.py:101
  120.5 4.5 %fusion.59 = f32[64,2048]{1,0:T(8,128)S(1)} fusion(s32[2048]{0:T(1024)S(1)} %dynamic_slice.39, f32[64,2048]{1,0:T(8,128)S(1)} %get-tuple-element.165, bf16[64,40960]{1,0:T(8,128)(2,1)} %get-tuple-element.174, s32[]{:T(128)S(6)} %select_n.263, pred[]{:T(512)S(6)} %compare.34), kind=kOutput, calls=%fused_computation.8.clone.1 | convolution fusion | flops 541327360 | bytes 1318917 | tf_op jit(solution)/shard_map/while/body/eval_jaxpr/dot_general | solution.py:101
  125.0 4.5 %fusion.59 = f32[64,2048]{1,0:T(8,128)S(1)} fusion(s32[2048]{0:T(1024)S(1)} %dynamic_slice.39, f32[64,2048]{1,0:T(8,128)S(1)} %get-tuple-element.165, bf16[64,40960]{1,0:T(8,128)(2,1)} %get-tuple-element.174, s32[]{:T(128)S(6)} %select_n.263, pred[]{:T(512)S(6)} %compare.34), kind=kOutput, calls=%fused_computation.8.clone.1 | convolution fusion | flops 541327360 | bytes 1318917 | tf_op jit(solution)/shard_map/while/body/eval_jaxpr/dot_general | solution.py:101
  129.5 4.5 %fusion.59 = f32[64,2048]{1,0:T(8,128)S(1)} fusion(s32[2048]{0:T(1024)S(1)} %dynamic_slice.39, f32[64,2048]{1,0:T(8,128)S(1)} %get-tuple-element.165, bf16[64,40960]{1,0:T(8,128)(2,1)} %get-tuple-element.174, s32[]{:T(128)S(6)} %select_n.263, pred[]{:T(512)S(6)} %compare.34), kind=kOutput, calls=%fused_computation.8.clone.1 | convolution fusion | flops 541327360 | bytes 1318917 | tf_op jit(solution)/shard_map/while/body/eval_jaxpr/dot_general | solution.py:101
  134.0 4.5 %fusion.59 = f32[64,2048]{1,0:T(8,128)S(1)} fusion(s32[2048]{0:T(1024)S(1)} %dynamic_slice.39, f32[64,2048]{1,0:T(8,128)S(1)} %get-tuple-element.165, bf16[64,40960]{1,0:T(8,128)(2,1)} %get-tuple-element.174, s32[]{:T(128)S(6)} %select_n.263, pred[]{:T(512)S(6)} %compare.34), kind=kOutput, calls=%fused_computation.8.clone.1 | convolution fusion | flops 541327360 | bytes 1318917 | tf_op jit(solution)/shard_map/while/body/eval_jaxpr/dot_general | solution.py:101
  138.6 4.5 %fusion.59 = f32[64,2048]{1,0:T(8,128)S(1)} fusion(s32[2048]{0:T(1024)S(1)} %dynamic_slice.39, f32[64,2048]{1,0:T(8,128)S(1)} %get-tuple-element.165, bf16[64,40960]{1,0:T(8,128)(2,1)} %get-tuple-element.174, s32[]{:T(128)S(6)} %select_n.263, pred[]{:T(512)S(6)} %compare.34), kind=kOutput, calls=%fused_computation.8.clone.1 | convolution fusion | flops 541327360 | bytes 1318917 | tf_op jit(solution)/shard_map/while/body/eval_jaxpr/dot_general | solution.py:101
  143.1 4.5 %fusion.59 = f32[64,2048]{1,0:T(8,128)S(1)} fusion(s32[2048]{0:T(1024)S(1)} %dynamic_slice.39, f32[64,2048]{1,0:T(8,128)S(1)} %get-tuple-element.165, bf16[64,40960]{1,0:T(8,128)(2,1)} %get-tuple-element.174, s32[]{:T(128)S(6)} %select_n.263, pred[]{:T(512)S(6)} %compare.34), kind=kOutput, calls=%fused_computation.8.clone.1 | convolution fusion | flops 541327360 | bytes 1318917 | tf_op jit(solution)/shard_map/while/body/eval_jaxpr/dot_general | solution.py:101
  147.6 4.5 %fusion.59 = f32[64,2048]{1,0:T(8,128)S(1)} fusion(s32[2048]{0:T(1024)S(1)} %dynamic_slice.39, f32[64,2048]{1,0:T(8,128)S(1)} %get-tuple-element.165, bf16[64,40960]{1,0:T(8,128)(2,1)} %get-tuple-element.174, s32[]{:T(128)S(6)} %select_n.263, pred[]{:T(512)S(6)} %compare.34), kind=kOutput, calls=%fused_computation.8.clone.1 | convolution fusion | flops 541327360 | bytes 1318917 | tf_op jit(solution)/shard_map/while/body/eval_jaxpr/dot_general | solution.py:101
  152.1 4.5 %fusion.59 = f32[64,2048]{1,0:T(8,128)S(1)} fusion(s32[2048]{0:T(1024)S(1)} %dynamic_slice.39, f32[64,2048]{1,0:T(8,128)S(1)} %get-tuple-element.165, bf16[64,40960]{1,0:T(8,128)(2,1)} %get-tuple-element.174, s32[]{:T(128)S(6)} %select_n.263, pred[]{:T(512)S(6)} %compare.34), kind=kOutput, calls=%fused_computation.8.clone.1 | convolution fusion | flops 541327360 | bytes 1318917 | tf_op jit(solution)/shard_map/while/body/eval_jaxpr/dot_general | solution.py:101
  156.6 0.7 convert_element_type.67
  157.7 14.4 %all-gather.2.cloned.1.call-done = bf16[4,2,32,2048]{3,2,1,0:T(8,128)(2,1)} async-done(((bf16[1,2,32,2048]{3,2,1,0:T(8,128)(2,1)}), bf16[4,2,32,2048]{3,2,1,0:T(8,128)(2,1)}) %all-gather.2.cloned.1.call-update) | async-done | bytes 1048592 | tf_op jit(solution)/shard_map/all_gather | solution.py:106
  172.1 1.4 reduce_sum.25
  173.5 67.5 %fusion.27 = bf16[2,8,2048]{2,1,0:T(8,128)(2,1)S(1)} fusion(s32[2048]{0:T(1024)S(1)} %add_select_fusion.6, pred[2048]{0:T(1024)(128)(4,1)S(1)} %fusion.36, bf16[2,32,2048]{2,1,0:T(8,128)(2,1)S(1)} %reduce_sum.25, s32[]{:T(128)S(6)} %select_n.186), kind=kOutput, calls=%fused_computation.40 | convolution fusion | flops 205619200 | bytes 141316 | tf_op jit(solution)/shard_map/dot_general | solution.py:108
  241.0 0.8 copy.19
  241.8 1.1 reshape.324
  242.8 12.2 %all_to_all.25 = bf16[8,2,2048]{2,1,0:T(2,128)(2,1)S(1)} all-to-all(bf16[8,2,2048]{2,1,0:T(2,128)(2,1)S(1)} %reshape.324), channel_id=1, replica_groups=mesh['blk'=8,'beam'=4] {'blk'}, dimensions={0} | all-to-all | bytes 131072 | tf_op jit(solution)/shard_map/all_to_all | solution.py:114
  255.0 1.2 reshape.325
  256.5 22.5 %fusion.23 = bf16[128,2,1152]{2,1,0:T(2,128)(2,1)} fusion(bf16[128,8,16,2]{1,3,0,2:T(2,128)(2,1)S(1)} %bitcast.52, bf16[128,8,16,1152]{3,2,1,0:T(8,128)(2,1)} %param.15), kind=kOutput, calls=%fused_computation.38 | convolution fusion | flops 75792384 | bytes 38404096 | tf_op jit(solution)/shard_map/mqtl,mqtp->mpl/dot_general | solution.py:117
  279.0 30.6 %all-reduce.2.cloned.1.call-done = bf16[128,2,1152]{2,1,0:T(2,128)(2,1)} async-done(((bf16[128,2,1152]{2,1,0:T(2,128)(2,1)}), bf16[128,2,1152]{2,1,0:T(2,128)(2,1)}) %all-reduce.2.cloned.1.call-update) | async-done | bytes 589840 | tf_op jit(solution)/shard_map/psum | solution.py:118
  309.6 1.7 dynamic-slice_convert_fusion
  (53 shorter events, 4.2 us)
Async XLA Ops:
  16.1 14.3 %all-to-all-start.1 = ((bf16[8,2,2560]{2,1,0:T(2,128)(2,1)}), bf16[8,2,2560]{2,1,0:T(2,128)(2,1)S(1)}, u32[]{:S(2)}, u32[]{:S(2)}) async-start(bf16[8,2,2560]{2,1,0:T(2,128)(2,1)} %reshape.322), calls=%async_computation.1 | async-start | bytes 163840 | tf_op jit(solution)/shard_map/all_to_all | solution.py:71
  30.5 10.9 %all-to-all-start = ((s32[1,8,5120]{2,0,1:T(1,128)}), s32[1,8,5120]{2,0,1:T(1,128)S(1)}, u32[]{:S(2)}, u32[]{:S(2)}) async-start(s32[1,8,5120]{2,0,1:T(1,128)} %copy.17), calls=%async_computation | async-start | bytes 327680 | tf_op jit(solution)/shard_map/all_to_all | solution.py:78
  33.9 138.2 %all-gather.2.cloned.1.call-start = ((), (), s32[]{:S(2)}) async-start(), calls=%async_computation.3 | async-start | bytes 1310720 | tf_op jit(solution)/shard_map/all_gather | solution.py:106
  157.4 152.2 %all-reduce.2.cloned.1.call-start = ((), (), s32[]{:S(2)}) async-start(), calls=%async_computation.4 | async-start | bytes 1179648 | tf_op jit(solution)/shard_map/psum | solution.py:118
Sparse Core Ops, SparseCore 0:
  157.5 14.5 all-gather.1
  279.1 30.3 all-reduce.1
